TPU v7x, 128 devices: a whole 4x4x4 slice. The times are simulated.
128 devices in a mesh: row: 32 (over z, y, core), col: 4 (over x).
Axes of the slice: x: 4, y: 4, z: 4, core: 2. Of those that a mesh axis runs over, the one named last changes fastest.
Arguments:
- tokens: bfloat16 [16384, 2048], P('row', 'col'), may hold values from -6 to 6
- cotangent: bfloat16 [16384, 2048], P('row', 'col'), may hold values from -6 to 6
- destination: int32 [16384], P('row'), may hold values from 0 to 16383, as said below
- segment_ids: int32 [16384], P('row'), may hold values from 0 to 7, as said below
- attn_gain: float32 [2048], replicated, may hold values from 0.5 to 1.5
- w_query: bfloat16 [2048, 2048], P('row', 'col'), may hold values from -0.125 to 0.125
- w_key: bfloat16 [2048, 256], P('row', 'col'), may hold values from -0.125 to 0.125
- w_value: bfloat16 [2048, 256], P('row', 'col'), may hold values from -0.125 to 0.125
- w_output: bfloat16 [2048, 2048], P('row', 'col'), may hold values from -0.5 to 0.5
- ffn_gain: float32 [2048], replicated, may hold values from 0.5 to 1.5
- w_gate: bfloat16 [2048, 5632], P('row', 'col'), may hold values from -0.125 to 0.125
- w_up: bfloat16 [2048, 5632], P('row', 'col'), may hold values from -0.125 to 0.125
- w_down: bfloat16 [2048, 5632], P('row', 'col'), may hold values from -0.078125 to 0.078125
Outputs:
- output: bfloat16 [16384, 2048], P('row', 'col')
- input_grad: bfloat16 [16384, 2048], P('row', 'col')
- attn_gain_grad: float32 [2048], P('row')
- w_query_grad: float32 [2048, 2048], P('row', 'col')
- w_key_grad: float32 [2048, 256], P('row', 'col')
- w_value_grad: float32 [2048, 256], P('row', 'col')
- w_output_grad: float32 [2048, 2048], P('row', 'col')
- ffn_gain_grad: float32 [2048], P('row')
- w_gate_grad: float32 [2048, 5632], P('row', 'col')
- w_up_grad: float32 [2048, 5632], P('row', 'col')
- w_down_grad: float32 [2048, 5632], P('row', 'col')
Inputs may be any that keep to these rules, and one draw needn't show every extreme that they name: `destination`: A permutation; the tokens of each aligned block of 512 arriving tokens go to exactly 16 places in each aligned block of 512 balanced places. `segment_ids`: within each aligned block of 512 places the ids start at 0 and rise by one where a new sequence begins, so a block holds at most 8 sequences; in every draw some block holds a single sequence of 512 tokens and some block holds 8 sequences.
All inputs are finite; a program needn't handle non-finite values.
Results may differ from a plain program's by a relative error of at most 0.028.
Values may be sent and summed in bfloat16 or wider, within the bound.
No kernel may reach another device: no remote copies, remote signals or barrier semaphores. Data moves between devices by JAX's collectives and lax.ppermute only.
A program may use at most 128 MiB of HBM per device.

v0:
```python
from functools import partial
import jax
import jax.numpy as jnp
from jax import lax
from jax.sharding import PartitionSpec as P

HEADS = 32
KV = 4
HD = 64
EPS = 1e-05
ROPE_BASE = 10000.0


def rope_tables(positions):
    half_width = HD // 2
    freqs = ROPE_BASE ** (-(jnp.arange(half_width, dtype=jnp.float32) * 2.0 / HD))
    angles = positions.astype(jnp.float32)[:, None] * freqs[None, :]
    return (jnp.cos(angles)[:, None, :], jnp.sin(angles)[:, None, :])


def rotate(values, cosine, sine):
    half_width = values.shape[-1] // 2
    first = values[..., :half_width]
    second = values[..., half_width:]
    return jnp.concatenate(
        [first * cosine - second * sine, second * cosine + first * sine], axis=-1
    )


def rotate_back(grads, cosine, sine):
    half_width = grads.shape[-1] // 2
    first = grads[..., :half_width]
    second = grads[..., half_width:]
    return jnp.concatenate(
        [first * cosine + second * sine, second * cosine - first * sine], axis=-1
    )


def positions_of(segment_ids):
    index = jnp.arange(segment_ids.shape[0], dtype=jnp.int32)
    change = jnp.concatenate([jnp.ones((1,), dtype=jnp.bool_), segment_ids[1:] != segment_ids[:-1]])
    starts = jnp.where(change, index, jnp.zeros_like(index))
    return index - lax.cummax(starts, axis=0)


def allowed_pairs(segment_ids):
    index = jnp.arange(segment_ids.shape[0], dtype=jnp.int32)
    return (segment_ids[:, None] == segment_ids[None, :]) & (index[None, :] <= index[:, None])


def rms_scale(values):
    return lax.rsqrt(jnp.mean(values * values, axis=-1, keepdims=True) + EPS)


def norm_back(values, inv_root, gain, grads):
    normed = values * inv_root
    scaled = grads * gain
    result = inv_root * (scaled - normed * jnp.mean(scaled * normed, axis=-1, keepdims=True))
    return (result, jnp.sum(grads * normed, axis=0))


def matmul(left, right):
    return jnp.dot(left, right, preferred_element_type=jnp.float32)


def head_scores(query_head, key_head, allowed, scale_factor):
    scores = matmul(query_head, key_head.T) * scale_factor
    return jnp.where(allowed, scores, -1e30)


def head_forward(inputs, key_heads, value_heads, allowed, scale_factor):
    query_head, kv_slot = inputs
    scores = head_scores(query_head, key_heads[kv_slot], allowed, scale_factor)
    peak = jnp.max(scores, axis=-1, keepdims=True)
    expo = jnp.exp(scores - peak)
    total = jnp.sum(expo, axis=-1, keepdims=True)
    probs = expo / total
    mixed = matmul(probs.astype(jnp.bfloat16), value_heads[kv_slot])
    return (mixed, (peak + jnp.log(total))[:, 0])


def head_backward(inputs, key_heads, value_heads, allowed, scale_factor):
    query_head, kv_slot, grad_head, log_total = inputs
    key_head = key_heads[kv_slot]
    value_head = value_heads[kv_slot]
    scores = head_scores(query_head, key_head, allowed, scale_factor)
    probs = jnp.exp(scores - log_total[:, None])
    prob_grad = matmul(grad_head, value_head.T)
    value_grad = matmul(probs.astype(jnp.bfloat16).T, grad_head)
    inner = jnp.sum(probs * prob_grad, axis=-1, keepdims=True)
    score_grad = (probs * (prob_grad - inner)).astype(jnp.bfloat16)
    query_grad = matmul(score_grad, key_head) * scale_factor
    key_grad = matmul(score_grad.T, query_head) * scale_factor
    return (query_grad, key_grad, value_grad)


def body(
    tokens,
    cotangent,
    destination,
    segment_ids,
    attn_gain,
    w_query,
    w_key,
    w_value,
    w_output,
    ffn_gain,
    w_gate,
    w_up,
    w_down,
):
    row_count = tokens.shape[0]
    quarter = tokens.shape[1]
    col_start = lax.axis_index("col") * quarter
    group_size = HEADS // KV
    send_order = jnp.argsort(destination)
    slot_ids = destination[send_order] % row_count
    arrived_rows, arrived_grads, arrived_slots = (
        lax.all_to_all(tokens[send_order], "row", split_axis=0, concat_axis=0, tiled=True),
        lax.all_to_all(cotangent[send_order], "row", split_axis=0, concat_axis=0, tiled=True),
        lax.all_to_all(slot_ids, "row", split_axis=0, concat_axis=0, tiled=True),
    )
    placing = jnp.argsort(arrived_slots)
    full_rows, full_grads = (
        lax.all_gather(arrived_rows[placing], "col", axis=1, tiled=True),
        lax.all_gather(arrived_grads[placing], "col", axis=1, tiled=True),
    )
    query_w, key_w, value_w, output_w = (
        lax.all_gather(w_query, "row", axis=0, tiled=True),
        lax.all_gather(w_key, "row", axis=0, tiled=True),
        lax.all_gather(w_value, "row", axis=0, tiled=True),
        lax.all_gather(w_output, "row", axis=0, tiled=True),
    )
    cosine, sine = rope_tables(positions_of(segment_ids))
    allowed = allowed_pairs(segment_ids)
    rows_wide = full_rows.astype(jnp.float32)
    inv_one = rms_scale(rows_wide)
    normed_one = (rows_wide * inv_one * attn_gain).astype(jnp.bfloat16)
    query = matmul(normed_one, query_w)
    key_raw = matmul(normed_one, key_w)
    value_raw = matmul(normed_one, value_w)
    query_heads_count = query.shape[1] // HD
    kv_count = key_raw.shape[1] // HD
    query_rot = (
        rotate(query.reshape(row_count, query_heads_count, HD), cosine, sine)
        .astype(jnp.bfloat16)
        .transpose(1, 0, 2)
    )
    key_rot = (
        rotate(key_raw.reshape(row_count, kv_count, HD), cosine, sine)
        .astype(jnp.bfloat16)
        .transpose(1, 0, 2)
    )
    value_heads = value_raw.astype(jnp.bfloat16).reshape(row_count, kv_count, HD).transpose(1, 0, 2)
    kv_slots = jnp.arange(query_heads_count, dtype=jnp.int32) // group_size
    scale_factor = HD ** (-0.5)
    mixed_heads, log_totals = lax.map(
        partial(
            head_forward,
            key_heads=key_rot,
            value_heads=value_heads,
            allowed=allowed,
            scale_factor=scale_factor,
        ),
        (query_rot, kv_slots),
    )
    mixed = (
        mixed_heads.transpose(1, 0, 2)
        .reshape(row_count, query_heads_count * HD)
        .astype(jnp.bfloat16)
    )
    attn_terms = matmul(mixed, output_w.T)
    attn_full = lax.psum(attn_terms, "col")
    resid = rows_wide + attn_full
    inv_two = rms_scale(resid)
    normed_two = (resid * inv_two * ffn_gain).astype(jnp.bfloat16)
    resid_part = lax.dynamic_slice_in_dim(resid, col_start, quarter, 1)
    gate_w, up_w, down_w = (
        lax.all_gather(w_gate, "row", axis=0, tiled=True),
        lax.all_gather(w_up, "row", axis=0, tiled=True),
        lax.all_gather(w_down, "row", axis=0, tiled=True),
    )
    gate = matmul(normed_two, gate_w)
    upper = matmul(normed_two, up_w)
    sigmoid_gate = jax.nn.sigmoid(gate)
    activ = (gate * sigmoid_gate * upper).astype(jnp.bfloat16)
    ffn_share = lax.psum_scatter(
        matmul(activ, down_w.T).astype(jnp.bfloat16), "col", scatter_dimension=1, tiled=True
    ).astype(jnp.float32)
    output_share = (resid_part + ffn_share).astype(jnp.bfloat16)
    gate_w, up_w, down_w = (
        lax.all_gather(w_gate, "row", axis=0, tiled=True),
        lax.all_gather(w_up, "row", axis=0, tiled=True),
        lax.all_gather(w_down, "row", axis=0, tiled=True),
    )
    down_weight_grad = matmul(full_grads.T, activ)
    act_grad = matmul(full_grads, down_w)
    gate_grad = (act_grad * upper * sigmoid_gate * (1.0 + gate * (1.0 - sigmoid_gate))).astype(
        jnp.bfloat16
    )
    up_grad = (act_grad * gate * sigmoid_gate).astype(jnp.bfloat16)
    gate_weight_grad = matmul(normed_two.T, gate_grad)
    up_weight_grad = matmul(normed_two.T, up_grad)
    normed_terms_two = matmul(gate_grad, gate_w.T) + matmul(up_grad, up_w.T)
    normed_grad_two = lax.psum(normed_terms_two, "col")
    resid_norm_grad, ffn_gain_grad = norm_back(resid, inv_two, ffn_gain, normed_grad_two)
    resid_grad = full_grads.astype(jnp.float32) + resid_norm_grad
    attn_grad_low = resid_grad.astype(jnp.bfloat16)
    ffn_results = (
        lax.psum_scatter(
            gate_weight_grad.astype(jnp.bfloat16), "row", scatter_dimension=0, tiled=True
        ).astype(jnp.float32),
        lax.psum_scatter(
            up_weight_grad.astype(jnp.bfloat16), "row", scatter_dimension=0, tiled=True
        ).astype(jnp.float32),
        lax.psum_scatter(
            down_weight_grad.astype(jnp.bfloat16), "row", scatter_dimension=0, tiled=True
        ).astype(jnp.float32),
        lax.psum_scatter(
            ffn_gain_grad.astype(jnp.bfloat16), "row", scatter_dimension=0, tiled=True
        ).astype(jnp.float32),
    )
    query_w, key_w, value_w, output_w = (
        lax.all_gather(w_query, "row", axis=0, tiled=True),
        lax.all_gather(w_key, "row", axis=0, tiled=True),
        lax.all_gather(w_value, "row", axis=0, tiled=True),
        lax.all_gather(w_output, "row", axis=0, tiled=True),
    )
    output_weight_grad = matmul(attn_grad_low.T, mixed)
    mixed_grad = matmul(attn_grad_low, output_w).astype(jnp.bfloat16)
    mixed_grad_heads = mixed_grad.reshape(row_count, query_heads_count, HD).transpose(1, 0, 2)
    query_grads, key_grads, value_grads = lax.map(
        partial(
            head_backward,
            key_heads=key_rot,
            value_heads=value_heads,
            allowed=allowed,
            scale_factor=scale_factor,
        ),
        (query_rot, kv_slots, mixed_grad_heads, log_totals),
    )
    query_grad = (
        rotate_back(query_grads.transpose(1, 0, 2), cosine, sine)
        .reshape(row_count, query_heads_count * HD)
        .astype(jnp.bfloat16)
    )
    key_sum = key_grads.reshape(kv_count, group_size, row_count, HD).sum(axis=1).transpose(1, 0, 2)
    key_grad = (
        rotate_back(key_sum, cosine, sine).reshape(row_count, kv_count * HD).astype(jnp.bfloat16)
    )
    value_sum = (
        value_grads.reshape(kv_count, group_size, row_count, HD).sum(axis=1).transpose(1, 0, 2)
    )
    value_grad = value_sum.reshape(row_count, kv_count * HD).astype(jnp.bfloat16)
    query_weight_grad = matmul(normed_one.T, query_grad)
    key_weight_grad = matmul(normed_one.T, key_grad)
    value_weight_grad = matmul(normed_one.T, value_grad)
    normed_terms_one = (
        matmul(query_grad, query_w.T) + matmul(key_grad, key_w.T) + matmul(value_grad, value_w.T)
    )
    normed_grad_one = lax.psum(normed_terms_one.astype(jnp.bfloat16), "col").astype(jnp.float32)
    rows_norm_grad, attn_gain_grad = norm_back(rows_wide, inv_one, attn_gain, normed_grad_one)
    rows_grad = resid_grad + rows_norm_grad
    input_share = lax.dynamic_slice_in_dim(rows_grad, col_start, quarter, 1).astype(jnp.bfloat16)
    attn_results = (
        lax.psum_scatter(
            query_weight_grad.astype(jnp.bfloat16), "row", scatter_dimension=0, tiled=True
        ).astype(jnp.float32),
        lax.psum_scatter(
            key_weight_grad.astype(jnp.bfloat16), "row", scatter_dimension=0, tiled=True
        ).astype(jnp.float32),
        lax.psum_scatter(
            value_weight_grad.astype(jnp.bfloat16), "row", scatter_dimension=0, tiled=True
        ).astype(jnp.float32),
        lax.psum_scatter(
            output_weight_grad.astype(jnp.bfloat16), "row", scatter_dimension=0, tiled=True
        ).astype(jnp.float32),
        lax.psum_scatter(
            attn_gain_grad.astype(jnp.bfloat16), "row", scatter_dimension=0, tiled=True
        ).astype(jnp.float32),
    )
    back_rows, back_grads = (
        lax.all_to_all(output_share[arrived_slots], "row", split_axis=0, concat_axis=0, tiled=True),
        lax.all_to_all(input_share[arrived_slots], "row", split_axis=0, concat_axis=0, tiled=True),
    )
    restore = jnp.argsort(send_order)
    return (
        back_rows[restore],
        back_grads[restore],
        attn_results[4],
        attn_results[0],
        attn_results[1],
        attn_results[2],
        attn_results[3],
        ffn_results[3],
        ffn_results[0],
        ffn_results[1],
        ffn_results[2],
    )


def solution(mesh):
    placed = (
        P("row", "col"),
        P("row", "col"),
        P("row"),
        P("row"),
        P(),
        P("row", "col"),
        P("row", "col"),
        P("row", "col"),
        P("row", "col"),
        P(),
        P("row", "col"),
        P("row", "col"),
        P("row", "col"),
    )
    return jax.shard_map(
        body,
        mesh=mesh,
        in_specs=placed,
        out_specs=(
            P("row", "col"),
            P("row", "col"),
            P("row"),
            P("row", "col"),
            P("row", "col"),
            P("row", "col"),
            P("row", "col"),
            P("row"),
            P("row", "col"),
            P("row", "col"),
            P("row", "col"),
        ),
        check_vma=False,
    )
```

profile of v0, /device:TPU:0, one launch (start us, length us, event | category | flops | bytes accessed | tf_op | source)
XLA Modules:
  0.0 1312.7 jit_solution(15525933860058886407)
XLA Ops:
  7.2 4.5 sort.45
  12.3 3.6 gather_fusion.1
  16.6 8.4 all-to-all-start.1
  25.0 2.6 gather_fusion
  27.7 4.6 all-to-all-done.1
  32.3 3.9 all-to-all-start
  37.6 3.8 sort.46
  41.4 6.6 all-to-all-done
  48.0 2.6 gather_fusion.2
  53.0 22.4 %all_gather.36 = bf16[2048,64]{1,0:T(8,128)(2,1)S(1)} all-gather(bf16[64,64]{1,0:T(8,128)(2,1)S(1)} %copy-done.22), channel_id=1, replica_groups=mesh['row'=32,'col'=4] {'row'}, dimensions={0}, use_global_device_ids=true | all-gather | bytes 270336 | tf_op jit(solution)/shard_map/all_gather | solution.py:130
  75.5 26.7 %all_gather.37 = bf16[2048,64]{1,0:T(8,128)(2,1)} all-gather(bf16[64,64]{1,0:T(8,128)(2,1)S(1)} %copy-done.23), channel_id=1, replica_groups=mesh['row'=32,'col'=4] {'row'}, dimensions={0}, use_global_device_ids=true | all-gather | bytes 270336 | tf_op jit(solution)/shard_map/all_gather | solution.py:131
  102.5 2.2 fusion.42
  104.8 2.4 convolution_bitcast_fusion.2
  107.7 2.5 fusion.43
  111.2 14.4 %all-gather.10.cloned.1.call-done = bf16[2048,512]{1,0:T(8,128)(2,1)} async-done(((bf16[64,512]{1,0:T(8,128)(2,1)}), bf16[2048,512]{1,0:T(8,128)(2,1)}) %all-gather.10.cloned.1.call-update) | async-done | bytes 2097168 | tf_op jit(solution)/shard_map/all_gather | solution.py:129
  125.6 3.0 fusion.73
  129.4 24.0 %while.32 = (s32[]{:T(128)}, bf16[8,512,64]{1,2,0:T(8,128)(2,1)S(1)}, f32[8,512]{1,0:T(8,128)}, bf16[8,512,64]{2,1,0:T(8,128)(2,1)S(1)}, bf16[1,512,64]{2,1,0:T(...) while((s32[]{:T(128)}, bf16[8,512,64]{1,2,0:T(8,128)(2,1)S(1)}, ...), condition=%wide.region_8.9_spmd.clone.clone, body=%wide.region_5.8_spmd.clone.sunk.clone | while | flops 69991936 | bytes 3695189 | solution.py:157
  153.4 17.8 %all-gather.12.cloned.1.call-done = bf16[2048,512]{1,0:T(8,128)(2,1)} async-done(((bf16[64,512]{1,0:T(8,128)(2,1)}), bf16[2048,512]{1,0:T(8,128)(2,1)}) %all-gather.12.cloned.1.call-update) | async-done | bytes 2097168 | tf_op jit(solution)/shard_map/all_gather | solution.py:132
  171.2 4.9 fusion.75
  177.4 2.6 gather_fusion.5
  180.0 17.1 %all_to_all.60 = bf16[32,16,512]{2,1,0:T(8,128)(2,1)S(1)} all-to-all(bf16[32,16,512]{2,1,0:T(8,128)(2,1)} %bitcast.194), channel_id=1, replica_groups=mesh['row'=32,'col'=4] {'row'}, dimensions={0} | all-to-all | bytes 1048576 | tf_op jit(solution)/shard_map/all_to_all | solution.py:120
  197.1 2.8 gather_fusion.6
  201.1 67.2 %all-reduce.7.cloned.1.call-done = f32[512,2048]{1,0:T(8,128)} async-done(((f32[512,2048]{1,0:T(8,128)}), f32[512,2048]{1,0:T(8,128)}) %all-reduce.7.cloned.1.call-update) | async-done | bytes 4194320 | tf_op jit(solution)/shard_map/psum | solution.py:173
  268.3 2.8 multiply_reduce_fusion.4
  271.1 2.0 copy-done.2
  274.8 44.2 %all-gather.14.cloned.1.call-done = bf16[2048,1408]{1,0:T(8,128)(2,1)} async-done(((bf16[64,1408]{1,0:T(8,128)(2,1)}), bf16[2048,1408]{1,0:T(8,128)(2,1)}) %all-gather.14.cloned.1.call-update) | async-done | bytes 5767184 | tf_op jit(solution)/shard_map/all_gather | solution.py:179
  319.0 8.3 fusion.76
  327.3 41.5 %all-gather.16.cloned.1.call-done = bf16[2048,1408]{1,0:T(8,128)(2,1)} async-done(((bf16[64,1408]{1,0:T(8,128)(2,1)}), bf16[2048,1408]{1,0:T(8,128)(2,1)}) %all-gather.16.cloned.1.call-update) | async-done | bytes 5767184 | tf_op jit(solution)/shard_map/all_gather | solution.py:180
  368.8 8.3 fusion.77
  377.1 23.9 %all-gather.22.cloned.1.call-done = bf16[512,2048]{1,0:T(8,128)(2,1)} async-done(((bf16[512,512]{1,0:T(8,128)(2,1)}), bf16[512,2048]{1,0:T(8,128)(2,1)}) %all-gather.22.cloned.1.call-update) | async-done | bytes 2097168 | tf_op jit(solution)/shard_map/all_gather | solution.py:126
  400.9 51.0 %all-gather.18.cloned.1.call-done = bf16[2048,1408]{1,0:T(8,128)(2,1)} async-done(((bf16[64,1408]{1,0:T(8,128)(2,1)}), bf16[2048,1408]{1,0:T(8,128)(2,1)}) %all-gather.18.cloned.1.call-update) | async-done | bytes 5767184 | tf_op jit(solution)/shard_map/all_gather | solution.py:181
  452.0 10.3 multiply_convert_fusion.3
  462.3 6.6 fusion.78
  468.9 5.1 convolution_add_fusion
  474.2 7.9 convolution_convert_fusion.5
  482.2 83.7 %all-reduce.9.cloned.1.call-done = f32[512,2048]{1,0:T(8,128)} async-done(((f32[512,2048]{1,0:T(8,128)}), f32[512,2048]{1,0:T(8,128)}) %all-reduce.9.cloned.1.call-update) | async-done | bytes 4194320 | tf_op jit(solution)/shard_map/psum | solution.py:205
  565.9 5.2 multiply_reduce_fusion.1
  571.8 2.8 multiply_add_fusion
  574.6 2.0 copy-done.4
  579.3 65.5 %while.33 = (s32[]{:T(128)}, f32[8,512,64]{1,2,0:T(8,128)}, f32[8,512,64]{1,2,0:T(8,128)}, f32[8,512,64]{1,2,0:T(8,128)}, bf16[8,512,64]{2,1,0:T(8,128)(2,1)}, /...) while((s32[]{:T(128)}, f32[8,512,64]{1,2,0:T(8,128)}, ...), condition=%wide.region_17.18_spmd.clone.clone, body=%wide.region_15.17_spmd.clone.sunk.clone | while | flops 170982912 | bytes 8996457 | solution.py:232
  602.0 1.9 fusion.161
  653.1 2.1 add_convert_fusion
  659.3 2.8 convolution_convert_fusion.4
  662.2 5.2 convolution_convert_fusion.3
  667.5 8.0 convolution_convert_fusion.2
  675.5 8.1 convolution_convert_fusion.1
  683.9 7.9 convolution_convert_fusion
  693.6 2.6 gather_fusion.3
  696.3 7.3 all-to-all-start.2
  703.5 10.4 all-reduce.11.cloned.1.call-done
  713.9 2.9 fusion.41
  718.4 2.6 gather_fusion.7
  721.0 7.3 all-to-all-start.4
  728.3 3.8 sort.47
  733.4 61.5 %reduce-scatter.13.cloned.1.call-done = bf16[64,64]{1,0:T(8,128)(2,1)} async-done(((bf16[2048,64]{1,0:T(8,128)(2,1)}), bf16[64,64]{1,0:T(8,128)(2,1)}) %reduce-scatter.13.cloned.1.call-update) | async-done | bytes 8208 | tf_op jit(solution)/shard_map/reduce_scatter | solution.py:269
  796.2 78.5 %reduce-scatter.15.cloned.1.call-done = bf16[64,64]{1,0:T(8,128)(2,1)} async-done(((bf16[2048,64]{1,0:T(8,128)(2,1)}), bf16[64,64]{1,0:T(8,128)(2,1)}) %reduce-scatter.15.cloned.1.call-update) | async-done | bytes 8208 | tf_op jit(solution)/shard_map/reduce_scatter | solution.py:272
  876.1 2.6 gather_fusion.4
  878.7 64.4 %all-reduce.2 = (bf16[2048]{0:T(1024)(128)(2,1)S(1)}, bf16[2048]{0:T(1024)(128)(2,1)S(1)}) all-reduce(bf16[2048]{0:T(1024)(128)(2,1)S(1)} %get-tuple-element.249, bf16[2048]{0:T(1024)(128)(2,1)S(1)} %copy-done.20), channel_id=5, replica_groups=mesh['row'=32,'col'=4] {'row'}, use_global_device_ids=true, to_apply=%region_23.24.clone | all-reduce | flops 4096 | bytes 16384
  943.7 2.6 gather_fusion.8
  946.4 10.0 reduce-scatter.11.cloned.1.call-done
  957.9 80.2 %reduce-scatter.17.cloned.1.call-done = bf16[64,512]{1,0:T(8,128)(2,1)} async-done(((bf16[2048,512]{1,0:T(8,128)(2,1)}), bf16[64,512]{1,0:T(8,128)(2,1)}) %reduce-scatter.17.cloned.1.call-update) | async-done | bytes 65552 | tf_op jit(solution)/shard_map/reduce_scatter | solution.py:275
  1039.6 86.9 %reduce-scatter.19.cloned.1.call-done = bf16[64,1408]{1,0:T(8,128)(2,1)} async-done(((bf16[2048,1408]{1,0:T(8,128)(2,1)}), bf16[64,1408]{1,0:T(8,128)(2,1)}) %reduce-scatter.19.cloned.1.call-update) | async-done | bytes 180240 | tf_op jit(solution)/shard_map/reduce_scatter | solution.py:210
  1128.2 87.2 %reduce-scatter.21.cloned.1.call-done = bf16[64,1408]{1,0:T(8,128)(2,1)} async-done(((bf16[2048,1408]{1,0:T(8,128)(2,1)}), bf16[64,1408]{1,0:T(8,128)(2,1)}) %reduce-scatter.21.cloned.1.call-update) | async-done | bytes 180240 | tf_op jit(solution)/shard_map/reduce_scatter | solution.py:213
  1217.0 86.7 %reduce-scatter.23.cloned.1.call-done = bf16[64,1408]{1,0:T(8,128)(2,1)} async-done(((bf16[2048,1408]{1,0:T(8,128)(2,1)}), bf16[64,1408]{1,0:T(8,128)(2,1)}) %reduce-scatter.23.cloned.1.call-update) | async-done | bytes 180240 | tf_op jit(solution)/shard_map/reduce_scatter | solution.py:216
  (266 shorter events, 130.7 us)
Async XLA Ops:
  7.2 17.9 %copy-start = (bf16[512,512]{1,0:T(8,128)(2,1)S(1)}, bf16[512,512]{1,0:T(8,128)(2,1)}, u32[]{:S(2)}) copy-start(bf16[512,512]{1,0:T(8,128)(2,1)} %param.17) | copy-start | bytes 1572868
  11.7 0.6 copy-start.27
  12.3 24.0 %copy-start.16 = (s32[1024]{0:T(1024)}, s32[1024]{0:T(1024)S(1)}, u32[]{:S(2)}) copy-start(s32[1024]{0:T(1024)S(1)} %pad_clamp_fusion.3) | copy-start | bytes 12292
  16.6 15.7 %all-to-all-start.1 = ((s32[32,16,1]{1,2,0:T(1,128)}), s32[32,16,1]{1,2,0:T(1,128)S(1)}, u32[]{:S(2)}, u32[]{:S(2)}) async-start(s32[32,16,1]{1,2,0:T(1,128)} %bitcast.2), calls=%async_computation.1 | async-start | bytes 32768 | tf_op jit(solution)/shard_map/all_to_all | solution.py:121
  27.7 24.6 %copy-start.26 = (s32[512]{0:T(512)S(1)}, s32[512]{0:T(512)}, u32[]{:S(2)}) copy-start(s32[512]{0:T(512)} %param.20) | copy-start | bytes 6148
  27.7 25.3 %copy-start.22 = (bf16[64,64]{1,0:T(8,128)(2,1)S(1)}, bf16[64,64]{1,0:T(8,128)(2,1)}, u32[]{:S(2)}) copy-start(bf16[64,64]{1,0:T(8,128)(2,1)} %param.23) | copy-start | bytes 24580
  27.7 47.8 %copy-start.23 = (bf16[64,64]{1,0:T(8,128)(2,1)S(1)}, bf16[64,64]{1,0:T(8,128)(2,1)}, u32[]{:S(2)}) copy-start(bf16[64,64]{1,0:T(8,128)(2,1)} %param.24) | copy-start | bytes 24580
  32.3 15.7 %all-to-all-start = ((bf16[32,16,512]{2,1,0:T(8,128)(2,1)}), bf16[32,16,512]{2,1,0:T(8,128)(2,1)S(1)}, u32[]{:S(2)}, u32[]{:S(2)}) async-start(bf16[32,16,512]{2,1,0:T(8,128)(2,1)} %bitcast), calls=%async_computation | async-start | bytes 1048576 | tf_op jit(solution)/shard_map/all_to_all | solution.py:119
  36.2 66.3 %all-gather.20.cloned.1.call-start = ((), (), s32[]{:S(2)}) async-start(), calls=%async_computation.29 | async-start | bytes 2621440 | tf_op jit(solution)/shard_map/all_gather | solution.py:125
  41.3 11.6 copy-start.21
  48.0 56.8 %copy-start.24 = (f32[2048]{0:T(1024)S(1)}, f32[2048]{0:T(1024)}, u32[]{:S(2)}) copy-start(f32[2048]{0:T(1024)} %param.21) | copy-start | bytes 24580
  50.6 75.0 %all-gather.10.cloned.1.call-start = ((), (), s32[]{:S(2)}) async-start(), calls=%async_computation.13 | async-start | bytes 2162688 | tf_op jit(solution)/shard_map/all_gather | solution.py:129
  51.4 119.8 %all-gather.12.cloned.1.call-start = ((), (), s32[]{:S(2)}) async-start(), calls=%async_computation.14 | async-start | bytes 2162688 | tf_op jit(solution)/shard_map/all_gather | solution.py:132
  52.1 216.2 %all-reduce.7.cloned.1.call-start = ((), (), s32[]{:S(2)}) async-start(), calls=%async_computation.15 | async-start | bytes 8388608 | tf_op jit(solution)/shard_map/psum | solution.py:173
  52.2 55.4 %copy-start.29 = (f32[32]{0:T(128)}, f32[32]{0:T(128)S(1)}, u32[]{:S(2)}) copy-start(f32[32]{0:T(128)S(1)} %negate_power_fusion) | copy-start | bytes 388
  53.0 54.5 %copy-start.15 = (f32[512]{0:T(512)}, f32[512]{0:T(512)S(1)}, u32[]{:S(2)}) copy-start(f32[512]{0:T(512)S(1)} %fusion.70) | copy-start | bytes 6148
  75.5 34.8 %copy-start.10 = (bf16[2048,64]{1,0:T(8,128)(2,1)}, bf16[2048,64]{1,0:T(8,128)(2,1)S(1)}, u32[]{:S(2)}) copy-start(bf16[2048,64]{1,0:T(8,128)(2,1)S(1)} %all_gather.36) | copy-start | bytes 786436
  102.5 5.2 copy-start.6
  104.8 2.8 copy-start.18
  153.4 22.7 %copy-start.9 = (bf16[8,512,64]{2,1,0:T(8,128)(2,1)}, bf16[8,512,64]{2,1,0:T(8,128)(2,1)S(1)}, u32[]{:S(2)}) copy-start(bf16[8,512,64]{2,1,0:T(8,128)(2,1)S(1)} %get-tuple-element.556) | copy-start | bytes 1572868
  176.1 1.2 copy-start.5
  176.1 1.3 copy-start.17
  176.1 142.8 %all-gather.14.cloned.1.call-start = ((), (), s32[]{:S(2)}) async-start(), calls=%async_computation.16 | async-start | bytes 5947392 | tf_op jit(solution)/shard_map/all_gather | solution.py:179
  176.7 192.1 %all-gather.16.cloned.1.call-start = ((), (), s32[]{:S(2)}) async-start(), calls=%async_computation.17 | async-start | bytes 5947392 | tf_op jit(solution)/shard_map/all_gather | solution.py:180
  177.3 223.6 %all-gather.22.cloned.1.call-start = ((), (), s32[]{:S(2)}) async-start(), calls=%async_computation.30 | async-start | bytes 2621440 | tf_op jit(solution)/shard_map/all_gather | solution.py:126
  180.0 88.3 %copy-start.7 = (bf16[512,2048]{1,0:T(8,128)(2,1)S(1)}, bf16[512,2048]{1,0:T(8,128)(2,1)}, u32[]{:S(2)}) copy-start(bf16[512,2048]{1,0:T(8,128)(2,1)} %all-gather.20.cloned.1.call-done) | copy-start | bytes 6291460
  199.9 252.1 %all-gather.18.cloned.1.call-start = ((), (), s32[]{:S(2)}) async-start(), calls=%async_computation.18 | async-start | bytes 5947392 | tf_op jit(solution)/shard_map/all_gather | solution.py:181
  200.6 72.4 %copy-start.14 = (f32[2048]{0:T(1024)S(1)}, f32[2048]{0:T(1024)}, u32[]{:S(2)}) copy-start(f32[2048]{0:T(1024)} %param.26) | copy-start | bytes 24580
  200.6 365.2 %all-reduce.9.cloned.1.call-start = ((), (), s32[]{:S(2)}) async-start(), calls=%async_computation.20 | async-start | bytes 8388608 | tf_op jit(solution)/shard_map/psum | solution.py:205
  271.1 2.0 copy-start.2
  462.3 6.6 copy-start.33
  462.3 6.6 copy-start.32
  462.3 6.6 copy-start.30
  474.0 218.0 %reduce-scatter.9.cloned.1.call-start = ((), (), s32[]{:S(2)}) async-start(), calls=%async_computation.19 | async-start | bytes 2621440 | tf_op jit(solution)/shard_map/reduce_scatter | solution.py:187
  482.1 231.8 %all-reduce.11.cloned.1.call-start = ((), (), s32[]{:S(2)}) async-start(), calls=%async_computation.21 | async-start | bytes 4194304 | tf_op jit(solution)/shard_map/psum | solution.py:261
  565.9 5.2 copy-start.3
  565.9 5.9 copy-start.8
  571.8 4.8 copy-start.12
  574.6 2.0 copy-start.4
  647.4 4.4 copy-start.11
  651.8 1.3 copy-start.13
  653.1 2.2 copy-start.19
  653.1 2.2 copy-start.25
  655.2 139.7 %reduce-scatter.13.cloned.1.call-start = ((), (), s32[]{:S(2)}) async-start(), calls=%async_computation.23 | async-start | bytes 540672 | tf_op jit(solution)/shard_map/reduce_scatter | solution.py:269
  657.1 217.6 %reduce-scatter.15.cloned.1.call-start = ((), (), s32[]{:S(2)}) async-start(), calls=%async_computation.24 | async-start | bytes 540672 | tf_op jit(solution)/shard_map/reduce_scatter | solution.py:272
  659.2 297.1 %reduce-scatter.11.cloned.1.call-start = ((), (), s32[]{:S(2)}) async-start(), calls=%async_computation.22 | async-start | bytes 2162688 | tf_op jit(solution)/shard_map/reduce_scatter | solution.py:266
  662.1 375.9 %reduce-scatter.17.cloned.1.call-start = ((), (), s32[]{:S(2)}) async-start(), calls=%async_computation.25 | async-start | bytes 2162688 | tf_op jit(solution)/shard_map/reduce_scatter | solution.py:275
  667.4 459.0 %reduce-scatter.19.cloned.1.call-start = ((), (), s32[]{:S(2)}) async-start(), calls=%async_computation.26 | async-start | bytes 5947392 | tf_op jit(solution)/shard_map/reduce_scatter | solution.py:210
  675.5 539.8 %reduce-scatter.21.cloned.1.call-start = ((), (), s32[]{:S(2)}) async-start(), calls=%async_computation.27 | async-start | bytes 5947392 | tf_op jit(solution)/shard_map/reduce_scatter | solution.py:213
  683.6 620.1 %reduce-scatter.23.cloned.1.call-start = ((), (), s32[]{:S(2)}) async-start(), calls=%async_computation.28 | async-start | bytes 5947392 | tf_op jit(solution)/shard_map/reduce_scatter | solution.py:216
  696.3 24.8 %all-to-all-start.2 = ((bf16[32,16,512]{2,1,0:T(8,128)(2,1)}), bf16[32,16,512]{2,1,0:T(8,128)(2,1)S(1)}, u32[]{:S(2)}, u32[]{:S(2)}) async-start(bf16[32,16,512]{2,1,0:T(8,128)(2,1)} %bitcast.14), calls=%async_computation.3 | async-start | bytes 1048576 | tf_op jit(solution)/shard_map/all_to_all | solution.py:283
  716.8 11.5 copy-start.28
  716.9 15.3 %copy-start.31 = (u32[128]{0:T(128)S(1)}, u32[128]{0:T(128)}, u32[]{:S(2)}) copy-start(u32[128]{0:T(128)} %constant.120) | copy-start | bytes 1540
  718.4 160.3 %copy-start.20 = (bf16[2048]{0:T(1024)(128)(2,1)S(1)}, bf16[2048]{0:T(1024)(128)(2,1)}, u32[]{:S(2)}) copy-start(bf16[2048]{0:T(1024)(128)(2,1)} %get-tuple-element.247) | copy-start | bytes 12292
  721.0 222.7 %all-to-all-start.4 = ((bf16[32,16,512]{2,1,0:T(8,128)(2,1)}), bf16[32,16,512]{2,1,0:T(8,128)(2,1)S(1)}, u32[]{:S(2)}, u32[]{:S(2)}) async-start(bf16[32,16,512]{2,1,0:T(8,128)(2,1)} %bitcast.24), calls=%async_computation.5 | async-start | bytes 1048576 | tf_op jit(solution)/shard_map/all_to_all | solution.py:284
  876.1 429.3 %copy-start.1 = (bf16[512,512]{1,0:T(8,128)(2,1)S(1)}, bf16[512,512]{1,0:T(8,128)(2,1)}, u32[]{:S(2)}) copy-start(bf16[512,512]{1,0:T(8,128)(2,1)} %param.17) | copy-start | bytes 1572868
Sparse Core Ops, SparseCore 0:
  50.7 28.4 all-gather.19
  81.5 44.0 all-gather.9
  127.9 43.2 all-gather.11
  176.2 91.9 all-reduce.6
  270.6 48.3 all-gather.13
  321.3 47.4 all-gather.15
  371.1 29.7 all-gather.21
  403.4 48.4 all-gather.17
  474.1 91.7 all-reduce.8
  568.1 29.5 reduce-scatter.8
  655.3 58.5 all-reduce.10
  717.8 77.0 reduce-scatter.12
  798.4 76.3 reduce-scatter.14
  878.2 78.1 reduce-scatter.10
  959.8 78.2 reduce-scatter.16
  1041.7 84.7 reduce-scatter.18
  1130.5 84.7 reduce-scatter.20
  1218.9 84.7 reduce-scatter.22
where the time goes:
time: 1320 us; the launch traced here: 1310 us
  waiting for transfers between devices  860 us (65%)
  matrix products  170 us (13%)
  blocking collectives  131 us (10%)
  other arithmetic  55.9 us (4%)
  local copies, waits for them, and re-layouts  51.2 us (4%)
  starting transfers between devices  28.6 us (2%)
  between operations  16 us (1%)
    dot_general x77, matrix products, matmul(): return jnp.dot(left, right, preferred_element_type=jnp.float32)  170 us
    reduce_scatter x1, waiting for transfers between devices, body(): lax.psum_scatter(up_weight_grad.astype(jnp.bfloat16), 'row', scatter_dime...  87.2 us
    reduce_scatter x1, waiting for transfers between devices, body(): lax.psum_scatter(gate_weight_grad.astype(jnp.bfloat16), 'row', scatter_di...  86.9 us
    reduce_scatter x1, waiting for transfers between devices, body(): lax.psum_scatter(down_weight_grad.astype(jnp.bfloat16), 'row', scatter_di...  86.7 us
    psum x1, waiting for transfers between devices, body(): normed_grad_two = lax.psum(normed_terms_two, 'col')  83.7 us
    reduce_scatter x1, waiting for transfers between devices, body(): lax.psum_scatter(output_weight_grad.astype(jnp.bfloat16), 'row', scatter_...  80.2 us
    reduce_scatter x1, waiting for transfers between devices, body(): lax.psum_scatter(value_weight_grad.astype(jnp.bfloat16), 'row', scatter_d...  78.5 us
    psum x1, waiting for transfers between devices, body(): attn_full = lax.psum(attn_terms, 'col')  67.2 us
  transfers between devices with their start and end apart: 22, of which 18 were waited for; matrix products, arithmetic and copies ran while one was open for 18% of the time, Pallas kernels for 0%

commit v1 on v0

--- a/solution.py
+++ b/solution.py
@@ -170,7 +170,10 @@
         .astype(jnp.bfloat16)
     )
     attn_terms = matmul(mixed, output_w.T)
-    attn_full = lax.psum(attn_terms, "col")
+    axis_n = lax.axis_size("col")
+    attn_full = attn_terms
+    for s in [[(dd, dd ^ nth) for dd in range(axis_n)] for nth in (1, 2, 4, 8, 16) if nth < axis_n]:
+        attn_full = attn_full + lax.ppermute(attn_full, "col", s)
     resid = rows_wide + attn_full
     inv_two = rms_scale(resid)
     normed_two = (resid * inv_two * ffn_gain).astype(jnp.bfloat16)

time: 1320 us -> 1270 us (0.962)
  waiting for transfers between devices: 860 us -> 803 us
    ppermute x0 -> x2, waiting for transfers between devices: none -> 191 us  [body(): attn_full = attn_full + lax.ppermute(attn_full, 'col', s)]
    psum x1 -> x0, waiting for transfers between devices: 67.2 us -> none  [body(): attn_full = lax.psum(attn_terms, 'col')]
    all_gather x1, waiting for transfers between devices: 51 us -> 0.01 us  [body(): lax.all_gather(w_down, 'row', axis=0, tiled=True)]
    all_gather x1, waiting for transfers between devices: 44.2 us -> 0.01 us  [body(): lax.all_gather(w_gate, 'row', axis=0, tiled=True)]
    all_gather x1, waiting for transfers between devices: 41.5 us -> 0.01 us  [body(): lax.all_gather(w_up, 'row', axis=0, tiled=True)]
    all_gather x1, waiting for transfers between devices: 23.9 us -> 0.01 us  [body(): lax.all_gather(arrived_grads[placing], 'col', axis=1, tiled=True)]
    all_gather x1, waiting for transfers between devices: 14.4 us -> 0.02 us  [body(): lax.all_gather(w_query, 'row', axis=0, tiled=True)]
  transfers between devices with their start and end apart: 22 -> 23, of which waited for: 18 -> 14; matrix products, arithmetic and copies ran while one was open for 18% -> 19% of each run, Pallas kernels for 0% -> 0%
where the time goes in v1:
time: 1270 us; the launch traced here: 1260 us
  waiting for transfers between devices  803 us (63%)
  matrix products  166 us (13%)
  blocking collectives  129 us (10%)
  other arithmetic  60.1 us (5%)
  local copies, waits for them, and re-layouts  50.5 us (4%)
  starting transfers between devices  33.1 us (3%)
  between operations  15.7 us (1%)
    ppermute x2, waiting for transfers between devices, body(): attn_full = attn_full + lax.ppermute(attn_full, 'col', s)  191 us
    dot_general x77, matrix products, matmul(): return jnp.dot(left, right, preferred_element_type=jnp.float32)  166 us
    reduce_scatter x1, waiting for transfers between devices, body(): lax.psum_scatter(gate_weight_grad.astype(jnp.bfloat16), 'row', scatter_di...  87.3 us
    reduce_scatter x1, waiting for transfers between devices, body(): lax.psum_scatter(down_weight_grad.astype(jnp.bfloat16), 'row', scatter_di...  87.1 us
    reduce_scatter x1, waiting for transfers between devices, body(): lax.psum_scatter(up_weight_grad.astype(jnp.bfloat16), 'row', scatter_dime...  86.7 us
    psum x1, waiting for transfers between devices, body(): normed_grad_two = lax.psum(normed_terms_two, 'col')  83.9 us
    reduce_scatter x1, waiting for transfers between devices, body(): lax.psum_scatter(output_weight_grad.astype(jnp.bfloat16), 'row', scatter_...  80.5 us
    reduce_scatter x1, waiting for transfers between devices, body(): lax.psum_scatter(value_weight_grad.astype(jnp.bfloat16), 'row', scatter_d...  78.8 us
  transfers between devices with their start and end apart: 23, of which 14 were waited for; matrix products, arithmetic and copies ran while one was open for 19% of the time, Pallas kernels for 0%

profile of v1, /device:TPU:0, one launch (start us, length us, event | category | flops | bytes accessed | tf_op | source)
XLA Modules:
  0.0 1256.8 jit_solution(2810117099235199229)
XLA Ops:
  7.2 4.5 sort.45
  12.3 3.6 gather_fusion.1
  16.6 8.4 all-to-all-start.1
  25.0 2.6 gather_fusion
  27.7 4.6 all-to-all-done.1
  32.3 3.9 all-to-all-start
  37.5 3.8 sort.46
  41.3 6.6 all-to-all-done
  48.0 2.6 gather_fusion.2
  52.2 2.0 gather_fusion.5
  54.2 15.4 %all_to_all.60 = bf16[32,16,512]{2,1,0:T(8,128)(2,1)S(1)} all-to-all(bf16[32,16,512]{2,1,0:T(8,128)(2,1)S(1)} %bitcast.195), channel_id=1, replica_groups=mesh['row'=32,'col'=4] {'row'}, dimensions={0} | all-to-all | bytes 1048576 | tf_op jit(solution)/shard_map/all_to_all | solution.py:120
  69.5 2.6 gather_fusion.6
  75.0 22.4 %all_gather.36 = bf16[2048,64]{1,0:T(8,128)(2,1)S(1)} all-gather(bf16[64,64]{1,0:T(8,128)(2,1)S(1)} %copy-done.19), channel_id=1, replica_groups=mesh['row'=32,'col'=4] {'row'}, dimensions={0}, use_global_device_ids=true | all-gather | bytes 270336 | tf_op jit(solution)/shard_map/all_gather | solution.py:130
  97.4 26.7 %all_gather.37 = bf16[2048,64]{1,0:T(8,128)(2,1)} all-gather(bf16[64,64]{1,0:T(8,128)(2,1)S(1)} %copy-done.20), channel_id=1, replica_groups=mesh['row'=32,'col'=4] {'row'}, dimensions={0}, use_global_device_ids=true | all-gather | bytes 270336 | tf_op jit(solution)/shard_map/all_gather | solution.py:131
  124.5 2.2 fusion.42
  126.7 2.4 convolution_bitcast_fusion.2
  129.7 2.5 fusion.43
  133.2 3.0 fusion.73
  136.9 24.1 %while.32 = (s32[]{:T(128)}, bf16[8,512,64]{1,2,0:T(8,128)(2,1)S(1)}, f32[8,512]{1,0:T(8,128)}, bf16[8,512,64]{2,1,0:T(8,128)(2,1)S(1)}, bf16[1,512,64]{2,1,0:T(...) while((s32[]{:T(128)}, bf16[8,512,64]{1,2,0:T(8,128)(2,1)S(1)}, ...), condition=%wide.region_8.9_spmd.clone.clone, body=%wide.region_5.8_spmd.clone.sunk.clone | while | flops 69991936 | bytes 3695189 | solution.py:157
  161.0 10.1 all-gather.12.cloned.1.call-done
  171.1 2.9 fusion.75
  175.6 108.1 %collective-permute-done = f32[512,2048]{1,0:T(8,128)S(1)} collective-permute-done((f32[512,2048]{1,0:T(8,128)S(1)}, f32[512,2048]{1,0:T(8,128)S(1)}, u32[]{:S(2)}, u32[]{:S(2)}) %collective-permute-start) | collective-permute-done | bytes 4194336 | tf_op jit(solution)/shard_map/ppermute | solution.py:176
  283.7 2.7 add.162
  286.4 3.4 collective-permute-start.1
  289.8 8.3 fusion.77
  298.1 82.4 %collective-permute-done.1 = f32[512,2048]{1,0:T(8,128)} collective-permute-done((f32[512,2048]{1,0:T(8,128)}, f32[512,2048]{1,0:T(8,128)}, u32[]{:S(2)}, u32[]{:S(2)}) %collective-permute-start.1) | collective-permute-done | bytes 4194336 | tf_op jit(solution)/shard_map/ppermute | solution.py:176
  380.6 4.2 multiply_reduce_fusion.4
  384.8 1.9 copy-done.2
  388.5 8.3 fusion.76
  396.8 10.7 multiply_convert_fusion.3
  407.5 3.5 fusion.78
  411.2 5.0 convolution_add_fusion
  416.5 7.9 convolution_convert_fusion.5
  424.5 83.9 %all-reduce.6.cloned.1.call-done = f32[512,2048]{1,0:T(8,128)} async-done(((f32[512,2048]{1,0:T(8,128)}), f32[512,2048]{1,0:T(8,128)}) %all-reduce.6.cloned.1.call-update) | async-done | bytes 4194320 | tf_op jit(solution)/shard_map/psum | solution.py:208
  508.4 5.2 multiply_reduce_fusion.1
  514.4 2.8 multiply_add_fusion
  517.2 2.0 copy-done.4
  521.8 65.5 %while.33 = (s32[]{:T(128)}, f32[8,512,64]{1,2,0:T(8,128)}, f32[8,512,64]{1,2,0:T(8,128)}, f32[8,512,64]{1,2,0:T(8,128)}, bf16[8,512,64]{2,1,0:T(8,128)(2,1)}, /...) while((s32[]{:T(128)}, f32[8,512,64]{1,2,0:T(8,128)}, ...), condition=%wide.region_16.17_spmd.clone.clone, body=%wide.region_14.16_spmd.clone.sunk.clone | while | flops 170982912 | bytes 8996457 | solution.py:235
  525.4 1.9 fusion.160
  544.5 1.9 fusion.161
  550.0 1.9 fusion.160
  595.7 2.1 add_convert_fusion
  601.8 2.8 convolution_convert_fusion.4
  604.7 5.2 convolution_convert_fusion.3
  609.9 8.0 convolution_convert_fusion.2
  618.0 8.1 convolution_convert_fusion.1
  626.4 7.9 convolution_convert_fusion
  636.1 2.6 gather_fusion.3
  638.7 7.3 all-to-all-start.2
  646.0 10.4 all-reduce.8.cloned.1.call-done
  656.4 2.9 fusion.41
  660.9 2.6 gather_fusion.7
  663.5 7.3 all-to-all-start.4
  670.8 3.8 sort.47
  675.9 62.0 %reduce-scatter.13.cloned.1.call-done = bf16[64,64]{1,0:T(8,128)(2,1)} async-done(((bf16[2048,64]{1,0:T(8,128)(2,1)}), bf16[64,64]{1,0:T(8,128)(2,1)}) %reduce-scatter.13.cloned.1.call-update) | async-done | bytes 8208 | tf_op jit(solution)/shard_map/reduce_scatter | solution.py:272
  739.2 78.8 %reduce-scatter.15.cloned.1.call-done = bf16[64,64]{1,0:T(8,128)(2,1)} async-done(((bf16[2048,64]{1,0:T(8,128)(2,1)}), bf16[64,64]{1,0:T(8,128)(2,1)}) %reduce-scatter.15.cloned.1.call-update) | async-done | bytes 8208 | tf_op jit(solution)/shard_map/reduce_scatter | solution.py:275
  819.3 2.6 gather_fusion.4
  822.0 64.1 %all-reduce.2 = (bf16[2048]{0:T(1024)(128)(2,1)S(1)}, bf16[2048]{0:T(1024)(128)(2,1)S(1)}) all-reduce(bf16[2048]{0:T(1024)(128)(2,1)S(1)} %get-tuple-element.249, bf16[2048]{0:T(1024)(128)(2,1)S(1)} %copy-done.18), channel_id=5, replica_groups=mesh['row'=32,'col'=4] {'row'}, use_global_device_ids=true, to_apply=%region_22.23.clone | all-reduce | flops 4096 | bytes 16384
  886.6 2.6 gather_fusion.8
  889.3 10.9 reduce-scatter.11.cloned.1.call-done
  901.7 80.5 %reduce-scatter.17.cloned.1.call-done = bf16[64,512]{1,0:T(8,128)(2,1)} async-done(((bf16[2048,512]{1,0:T(8,128)(2,1)}), bf16[64,512]{1,0:T(8,128)(2,1)}) %reduce-scatter.17.cloned.1.call-update) | async-done | bytes 65552 | tf_op jit(solution)/shard_map/reduce_scatter | solution.py:278
  983.7 87.3 %reduce-scatter.19.cloned.1.call-done = bf16[64,1408]{1,0:T(8,128)(2,1)} async-done(((bf16[2048,1408]{1,0:T(8,128)(2,1)}), bf16[64,1408]{1,0:T(8,128)(2,1)}) %reduce-scatter.19.cloned.1.call-update) | async-done | bytes 180240 | tf_op jit(solution)/shard_map/reduce_scatter | solution.py:213
  1072.7 86.7 %reduce-scatter.21.cloned.1.call-done = bf16[64,1408]{1,0:T(8,128)(2,1)} async-done(((bf16[2048,1408]{1,0:T(8,128)(2,1)}), bf16[64,1408]{1,0:T(8,128)(2,1)}) %reduce-scatter.21.cloned.1.call-update) | async-done | bytes 180240 | tf_op jit(solution)/shard_map/reduce_scatter | solution.py:216
  1161.0 87.1 %reduce-scatter.23.cloned.1.call-done = bf16[64,1408]{1,0:T(8,128)(2,1)} async-done(((bf16[2048,1408]{1,0:T(8,128)(2,1)}), bf16[64,1408]{1,0:T(8,128)(2,1)}) %reduce-scatter.23.cloned.1.call-update) | async-done | bytes 180240 | tf_op jit(solution)/shard_map/reduce_scatter | solution.py:219
  (264 shorter events, 128.2 us)
Async XLA Ops:
  7.2 17.9 %copy-start = (bf16[512,512]{1,0:T(8,128)(2,1)S(1)}, bf16[512,512]{1,0:T(8,128)(2,1)}, u32[]{:S(2)}) copy-start(bf16[512,512]{1,0:T(8,128)(2,1)} %param.17) | copy-start | bytes 1572868
  11.7 0.6 copy-start.24
  16.6 15.7 %all-to-all-start.1 = ((s32[32,16,1]{1,2,0:T(1,128)}), s32[32,16,1]{1,2,0:T(1,128)S(1)}, u32[]{:S(2)}, u32[]{:S(2)}) async-start(s32[32,16,1]{1,2,0:T(1,128)} %bitcast.2), calls=%async_computation.1 | async-start | bytes 32768 | tf_op jit(solution)/shard_map/all_to_all | solution.py:121
  27.7 24.5 %copy-start.5 = (bf16[512,512]{1,0:T(8,128)(2,1)S(1)}, bf16[512,512]{1,0:T(8,128)(2,1)}, u32[]{:S(2)}) copy-start(bf16[512,512]{1,0:T(8,128)(2,1)} %param.18) | copy-start | bytes 1572868
  32.3 15.7 %all-to-all-start = ((bf16[32,16,512]{2,1,0:T(8,128)(2,1)}), bf16[32,16,512]{2,1,0:T(8,128)(2,1)S(1)}, u32[]{:S(2)}, u32[]{:S(2)}) async-start(bf16[32,16,512]{2,1,0:T(8,128)(2,1)} %bitcast), calls=%async_computation | async-start | bytes 1048576 | tf_op jit(solution)/shard_map/all_to_all | solution.py:119
  36.2 88.2 %all-gather.20.cloned.1.call-start = ((), (), s32[]{:S(2)}) async-start(), calls=%async_computation.28 | async-start | bytes 2621440 | tf_op jit(solution)/shard_map/all_gather | solution.py:125
  50.6 82.6 %all-gather.10.cloned.1.call-start = ((), (), s32[]{:S(2)}) async-start(), calls=%async_computation.13 | async-start | bytes 2162688 | tf_op jit(solution)/shard_map/all_gather | solution.py:129
  51.4 119.8 %all-gather.12.cloned.1.call-start = ((), (), s32[]{:S(2)}) async-start(), calls=%async_computation.14 | async-start | bytes 2162688 | tf_op jit(solution)/shard_map/all_gather | solution.py:132
  52.1 237.7 %all-gather.22.cloned.1.call-start = ((), (), s32[]{:S(2)}) async-start(), calls=%async_computation.29 | async-start | bytes 2621440 | tf_op jit(solution)/shard_map/all_gather | solution.py:126
  54.1 20.1 %copy-start.23 = (s32[512]{0:T(512)S(1)}, s32[512]{0:T(512)}, u32[]{:S(2)}) copy-start(s32[512]{0:T(512)} %param.20) | copy-start | bytes 6148
  54.1 20.8 %copy-start.19 = (bf16[64,64]{1,0:T(8,128)(2,1)S(1)}, bf16[64,64]{1,0:T(8,128)(2,1)}, u32[]{:S(2)}) copy-start(bf16[64,64]{1,0:T(8,128)(2,1)} %param.23) | copy-start | bytes 24580
  54.2 43.3 %copy-start.20 = (bf16[64,64]{1,0:T(8,128)(2,1)S(1)}, bf16[64,64]{1,0:T(8,128)(2,1)}, u32[]{:S(2)}) copy-start(bf16[64,64]{1,0:T(8,128)(2,1)} %param.24) | copy-start | bytes 24580
  69.5 57.2 %copy-start.21 = (f32[2048]{0:T(1024)S(1)}, f32[2048]{0:T(1024)}, u32[]{:S(2)}) copy-start(f32[2048]{0:T(1024)} %param.21) | copy-start | bytes 24580
  72.2 217.6 %all-gather.18.cloned.1.call-start = ((), (), s32[]{:S(2)}) async-start(), calls=%async_computation.17 | async-start | bytes 5947392 | tf_op jit(solution)/shard_map/all_gather | solution.py:184
  72.8 315.7 %all-gather.16.cloned.1.call-start = ((), (), s32[]{:S(2)}) async-start(), calls=%async_computation.16 | async-start | bytes 5947392 | tf_op jit(solution)/shard_map/all_gather | solution.py:183
  73.3 323.4 %all-gather.14.cloned.1.call-start = ((), (), s32[]{:S(2)}) async-start(), calls=%async_computation.15 | async-start | bytes 5947392 | tf_op jit(solution)/shard_map/all_gather | solution.py:182
  74.1 434.4 %all-reduce.6.cloned.1.call-start = ((), (), s32[]{:S(2)}) async-start(), calls=%async_computation.19 | async-start | bytes 8388608 | tf_op jit(solution)/shard_map/psum | solution.py:208
  74.1 55.3 %copy-start.26 = (f32[32]{0:T(128)}, f32[32]{0:T(128)S(1)}, u32[]{:S(2)}) copy-start(f32[32]{0:T(128)S(1)} %negate_power_fusion) | copy-start | bytes 388
  75.0 54.5 %copy-start.15 = (f32[512]{0:T(512)}, f32[512]{0:T(512)S(1)}, u32[]{:S(2)}) copy-start(f32[512]{0:T(512)S(1)} %fusion.70) | copy-start | bytes 6148
  97.4 34.8 %copy-start.10 = (bf16[2048,64]{1,0:T(8,128)(2,1)}, bf16[2048,64]{1,0:T(8,128)(2,1)S(1)}, u32[]{:S(2)}) copy-start(bf16[2048,64]{1,0:T(8,128)(2,1)S(1)} %all_gather.36) | copy-start | bytes 786436
  124.5 5.2 copy-start.6
  126.7 2.8 copy-start.16
  161.0 13.1 %copy-start.9 = (bf16[8,512,64]{2,1,0:T(8,128)(2,1)}, bf16[8,512,64]{2,1,0:T(8,128)(2,1)S(1)}, u32[]{:S(2)}) copy-start(bf16[8,512,64]{2,1,0:T(8,128)(2,1)S(1)} %get-tuple-element.554) | copy-start | bytes 1572868
  174.0 109.7 %collective-permute-start = (f32[512,2048]{1,0:T(8,128)S(1)}, f32[512,2048]{1,0:T(8,128)S(1)}, u32[]{:S(2)}, u32[]{:S(2)}) collective-permute-start(f32[512,2048]{1,0:T(8,128)S(1)} %fusion.75), channel_id=1, source_target_pairs={{0,1},{1,0},{2,3},{3,2},{4,5},{5,4},{6,7},{7,6},{8,9},{9,8},{10,11... | collective-permute-start | bytes 12582920 | tf_op jit(solution)/shard_map/ppermute | solution.py:176
  286.4 94.1 %copy-start.7 = (bf16[512,2048]{1,0:T(8,128)(2,1)S(1)}, bf16[512,2048]{1,0:T(8,128)(2,1)}, u32[]{:S(2)}) copy-start(bf16[512,2048]{1,0:T(8,128)(2,1)} %all-gather.20.cloned.1.call-done) | copy-start | bytes 6291460
  286.4 94.1 %collective-permute-start.1 = (f32[512,2048]{1,0:T(8,128)}, f32[512,2048]{1,0:T(8,128)}, u32[]{:S(2)}, u32[]{:S(2)}) collective-permute-start(f32[512,2048]{1,0:T(8,128)} %add.162), channel_id=1, source_target_pairs={{0,2},{1,3},{2,0},{3,1},{4,6},{5,7},{6,4},{7,5},{8,10},{9,11},{10,... | collective-permute-start | bytes 12582920 | tf_op jit(solution)/shard_map/ppermute | solution.py:176
  298.1 88.6 %copy-start.14 = (f32[2048]{0:T(1024)S(1)}, f32[2048]{0:T(1024)}, u32[]{:S(2)}) copy-start(f32[2048]{0:T(1024)} %param.26) | copy-start | bytes 24580
  384.8 2.0 copy-start.2
  396.8 10.7 copy-start.28
  407.5 3.5 copy-start.31
  407.5 3.5 copy-start.30
  407.5 3.7 copy-start.27
  416.3 218.2 %reduce-scatter.9.cloned.1.call-start = ((), (), s32[]{:S(2)}) async-start(), calls=%async_computation.18 | async-start | bytes 2621440 | tf_op jit(solution)/shard_map/reduce_scatter | solution.py:190
  424.5 232.0 %all-reduce.8.cloned.1.call-start = ((), (), s32[]{:S(2)}) async-start(), calls=%async_computation.20 | async-start | bytes 4194304 | tf_op jit(solution)/shard_map/psum | solution.py:264
  508.4 5.2 copy-start.3
  508.4 5.9 copy-start.8
  514.4 4.8 copy-start.12
  517.2 2.0 copy-start.4
  589.9 4.4 copy-start.11
  594.3 1.3 copy-start.13
  595.7 2.2 copy-start.17
  595.7 2.2 copy-start.22
  597.8 140.1 %reduce-scatter.13.cloned.1.call-start = ((), (), s32[]{:S(2)}) async-start(), calls=%async_computation.22 | async-start | bytes 540672 | tf_op jit(solution)/shard_map/reduce_scatter | solution.py:272
  599.7 218.3 %reduce-scatter.15.cloned.1.call-start = ((), (), s32[]{:S(2)}) async-start(), calls=%async_computation.23 | async-start | bytes 540672 | tf_op jit(solution)/shard_map/reduce_scatter | solution.py:275
  601.8 298.4 %reduce-scatter.11.cloned.1.call-start = ((), (), s32[]{:S(2)}) async-start(), calls=%async_computation.21 | async-start | bytes 2162688 | tf_op jit(solution)/shard_map/reduce_scatter | solution.py:269
  604.6 377.6 %reduce-scatter.17.cloned.1.call-start = ((), (), s32[]{:S(2)}) async-start(), calls=%async_computation.24 | async-start | bytes 2162688 | tf_op jit(solution)/shard_map/reduce_scatter | solution.py:278
  609.9 461.1 %reduce-scatter.19.cloned.1.call-start = ((), (), s32[]{:S(2)}) async-start(), calls=%async_computation.25 | async-start | bytes 5947392 | tf_op jit(solution)/shard_map/reduce_scatter | solution.py:213
  617.9 541.4 %reduce-scatter.21.cloned.1.call-start = ((), (), s32[]{:S(2)}) async-start(), calls=%async_computation.26 | async-start | bytes 5947392 | tf_op jit(solution)/shard_map/reduce_scatter | solution.py:216
  626.1 622.0 %reduce-scatter.23.cloned.1.call-start = ((), (), s32[]{:S(2)}) async-start(), calls=%async_computation.27 | async-start | bytes 5947392 | tf_op jit(solution)/shard_map/reduce_scatter | solution.py:219
  638.7 24.8 %all-to-all-start.2 = ((bf16[32,16,512]{2,1,0:T(8,128)(2,1)}), bf16[32,16,512]{2,1,0:T(8,128)(2,1)S(1)}, u32[]{:S(2)}, u32[]{:S(2)}) async-start(bf16[32,16,512]{2,1,0:T(8,128)(2,1)} %bitcast.194), calls=%async_computation.3 | async-start | bytes 1048576 | tf_op jit(solution)/shard_map/all_to_all | solution.py:286
  659.3 11.5 copy-start.25
  659.4 15.2 %copy-start.29 = (u32[128]{0:T(128)S(1)}, u32[128]{0:T(128)}, u32[]{:S(2)}) copy-start(u32[128]{0:T(128)} %constant.120) | copy-start | bytes 1540
  660.9 161.1 %copy-start.18 = (bf16[2048]{0:T(1024)(128)(2,1)S(1)}, bf16[2048]{0:T(1024)(128)(2,1)}, u32[]{:S(2)}) copy-start(bf16[2048]{0:T(1024)(128)(2,1)} %get-tuple-element.247) | copy-start | bytes 12292
  663.5 223.1 %all-to-all-start.4 = ((bf16[32,16,512]{2,1,0:T(8,128)(2,1)}), bf16[32,16,512]{2,1,0:T(8,128)(2,1)S(1)}, u32[]{:S(2)}, u32[]{:S(2)}) async-start(bf16[32,16,512]{2,1,0:T(8,128)(2,1)} %bitcast.24), calls=%async_computation.5 | async-start | bytes 1048576 | tf_op jit(solution)/shard_map/all_to_all | solution.py:287
  819.3 430.5 %copy-start.1 = (bf16[512,512]{1,0:T(8,128)(2,1)S(1)}, bf16[512,512]{1,0:T(8,128)(2,1)}, u32[]{:S(2)}) copy-start(bf16[512,512]{1,0:T(8,128)(2,1)} %param.17) | copy-start | bytes 1572868
Sparse Core Ops, SparseCore 0:
  50.7 28.4 all-gather.19
  81.5 44.2 all-gather.9
  128.1 42.9 all-gather.11
  173.2 46.0 all-gather.21
  221.4 49.4 all-gather.17
  273.0 47.4 all-gather.15
  322.7 47.4 all-gather.13
  416.4 92.0 all-reduce.5
  511.0 29.4 reduce-scatter.8
  597.9 58.4 all-reduce.7
  660.8 77.0 reduce-scatter.12
  741.6 76.3 reduce-scatter.14
  822.0 78.1 reduce-scatter.10
  904.0 78.1 reduce-scatter.16
  986.3 84.7 reduce-scatter.18
  1074.6 84.6 reduce-scatter.20
  1163.4 84.6 reduce-scatter.22
